TPU v7x, 32 devices: a whole 2x2x4 slice. The times are simulated.
32 devices in a mesh: groups: 2 (over y), ctx: 4 (over z), head: 2 (over x), tp: 2 (over core).
Axes of the slice: x: 2, y: 2, z: 4, core: 2. Of those that a mesh axis runs over, the one named last changes fastest.
Arguments:
- queries: bfloat16 [32, 2048, 128], P(('head', 'tp'), ('groups', 'ctx')), parts along dimension 1, may hold values from -80 to 80
- stretch_keys: bfloat16 [8, 2048, 128], P(('head', 'tp'), ('groups', 'ctx')), parts along dimension 1, may hold values from -120 to 120
- stretch_values: bfloat16 [8, 2048, 128], P(('head', 'tp'), ('groups', 'ctx')), parts along dimension 1, may hold values from -6 to 6
- cache_keys: bfloat16 [8, 32768, 128], P(('head', 'tp'), ('groups', 'ctx')), parts along dimension 1, may hold values from -6 to 6
- cache_values: bfloat16 [8, 32768, 128], P(('head', 'tp'), ('groups', 'ctx')), parts along dimension 1, may hold values from -6 to 6
- block_picks: int32 [4, 8, 16], P('groups'), parts along dimension 0, may hold values from 0 to 31, as said below
- block_table: int32 [64], P('groups'), parts along dimension 0, may hold values from 0 to 31, as said below
Outputs:
- attended: bfloat16 [32, 2048, 128], P(('head', 'tp'), ('groups', 'ctx')), parts along dimension 1
There are 2 independent parts, one for each index of `groups`. A program takes and returns all parts, laid end to end along the dimension named above; each array names one. Nothing has to cross between parts.
Inputs may be any that keep to these rules, and one draw needn't show every extreme that they name: `block_picks`: for each query block and KV head the 16 picks are different logical blocks; exactly 4 of them have slots on each of 4 different indices of ctx, slot s lying on index s // 8. `block_table`: A permutation of the 32 physical slots.
All inputs are finite; a program needn't handle non-finite values.
Results may differ from a plain program's by a relative error of at most 0.0032.
Values may be sent and summed in bfloat16 or wider, within the bound.
No kernel may reach another device: no remote copies, remote signals or barrier semaphores. Data moves between devices by JAX's collectives and lax.ppermute only.
A program may use at most 64 MiB of HBM per device.

v0:
```python
import jax
import jax.numpy as jnp
import numpy as np
from jax import lax
from jax.sharding import PartitionSpec as P

BLOCK = 512
TOPK = 16


def shifted(value, axis, by):
    count = lax.axis_size(axis)
    pairs = [(i, i + by) for i in range(count) if 0 <= i + by < count]
    return lax.ppermute(value, axis, pairs)


def as_sent(value):

    def short(part):
        return part.astype(jnp.bfloat16) if part.dtype == jnp.float32 else part

    return jax.tree.map(short, value)


def partner(value, axis, bit):
    mask = 2**bit
    pairs = [(source, source ^ mask) for source in range(lax.axis_size(axis))]
    return lax.ppermute(value, axis, pairs)


def lookup(lookup_table, indices):
    entries = jnp.arange(lookup_table.shape[0], dtype=jnp.int32)
    return jnp.sum(jnp.where(indices[..., None] == entries, lookup_table, 0), axis=-1)


def owner_rank(owners):
    ordinal = jnp.arange(owners.shape[-1], dtype=jnp.int32)
    before = (owners[..., :, None] == owners[..., None, :]) & (ordinal[None, :] < ordinal[:, None])
    return jnp.sum(before, axis=-1)


def pick_rows(source, indices):
    return source[indices]


def take_blocks(blocks, indices):
    return jax.vmap(pick_rows)(blocks, indices)


def attend(query_rows, all_keys, all_values, allowed_mask):
    tile_relevance = jnp.einsum(
        "rd,kd->rk", query_rows, all_keys, preferred_element_type=jnp.float32
    )
    tile_relevance = tile_relevance * query_rows.shape[-1] ** (-0.5)
    tile_relevance = jnp.where(allowed_mask, tile_relevance, -jnp.inf)
    row_max = jnp.max(tile_relevance, axis=-1, keepdims=True)
    weights = jnp.exp(tile_relevance - row_max)
    weight_sum = jnp.sum(weights, axis=-1, keepdims=True)
    mixed = jnp.einsum(
        "rk,kd->rd", weights.astype(jnp.bfloat16), all_values, preferred_element_type=jnp.float32
    )
    return (mixed / weight_sum).astype(jnp.bfloat16)


def shards(
    queries, stretch_keys, stretch_values, cache_keys, cache_values, block_picks, block_table
):
    kv_dev, tok_dev, head_dim = stretch_keys.shape
    q_per_kv = queries.shape[0] // kv_dev
    blocks_dev = cache_keys.shape[1] // BLOCK
    ctx_size = lax.axis_size("ctx")
    ctx_index = lax.axis_index("ctx")
    per_peer = max(1, TOPK // ctx_size)
    parity = ctx_index % 2
    head_ids = lax.axis_index(("head", "tp")) * kv_dev + jnp.arange(kv_dev, dtype=jnp.int32)
    selector = head_ids[:, None] == jnp.arange(block_picks.shape[1], dtype=jnp.int32)[None, :]
    my_picks = jnp.sum(jnp.where(selector[None, :, :, None], block_picks[:, None, :, :], 0), axis=2)
    physical = lookup(block_table, my_picks)
    owners = physical // blocks_dev
    in_owner = physical % blocks_dev
    peer_rank = owner_rank(owners)
    targets = np.arange(ctx_size) * tok_dev // BLOCK
    target_owner = owners[targets]
    target_rank = peer_rank[targets]
    target_local = in_owner[targets]
    slot_ids = jnp.arange(per_peer, dtype=jnp.int32)
    matched = (target_owner[:, :, None, :] == ctx_index) & (
        target_rank[:, :, None, :] == slot_ids[None, None, :, None]
    )
    chosen = jnp.sum(jnp.where(matched, target_local[:, :, None, :], 0), axis=-1)
    usable = jnp.any(matched, axis=-1)
    chosen = jnp.transpose(chosen, (1, 0, 2)).reshape(kv_dev, ctx_size * per_peer)
    usable = jnp.transpose(usable, (1, 0, 2)).reshape(kv_dev, ctx_size * per_peer)
    my_block = ctx_index * tok_dev // BLOCK
    my_owner = lax.dynamic_index_in_dim(owners, my_block, 0, keepdims=False)
    my_rank = lax.dynamic_index_in_dim(peer_rank, my_block, 0, keepdims=False)
    my_slot = my_owner * per_peer + my_rank
    prev_keys, prev_values = shifted((stretch_keys, stretch_values), "ctx", 1)
    half_rows = BLOCK // 2
    key_halves = cache_keys.reshape(kv_dev, blocks_dev * 2, half_rows, head_dim)
    value_halves = cache_values.reshape(kv_dev, blocks_dev * 2, half_rows, head_dim)
    row_side = jnp.asarray(np.repeat(np.arange(ctx_size) % 2, per_peer), jnp.int32)
    half_index = chosen * 2 + row_side[None, :]
    sent_keys = jnp.where(usable[:, :, None, None], take_blocks(key_halves, half_index), 0).astype(
        jnp.bfloat16
    )
    sent_values = jnp.where(
        usable[:, :, None, None], take_blocks(value_halves, half_index), 0
    ).astype(jnp.bfloat16)
    got_keys, got_values = (
        lax.all_to_all(sent_keys, "ctx", split_axis=1, concat_axis=1, tiled=True),
        lax.all_to_all(sent_values, "ctx", split_axis=1, concat_axis=1, tiled=True),
    )
    mine_keys = take_blocks(got_keys, my_slot)
    mine_values = take_blocks(got_values, my_slot)
    other_keys, other_values = (
        partner(as_sent(mine_keys), "ctx", 0).astype(mine_keys.dtype),
        partner(as_sent(mine_values), "ctx", 0).astype(mine_values.dtype),
    )
    first_keys = jnp.where(parity == 0, mine_keys, other_keys)
    second_keys = jnp.where(parity == 0, other_keys, mine_keys)
    first_values = jnp.where(parity == 0, mine_values, other_values)
    second_values = jnp.where(parity == 0, other_values, mine_values)
    live_keys = jnp.concatenate([first_keys, second_keys], axis=2)
    live_values = jnp.concatenate([first_values, second_values], axis=2)
    span_cols = TOPK * BLOCK
    live_keys = live_keys.reshape(kv_dev, span_cols, head_dim)
    live_values = live_values.reshape(kv_dev, span_cols, head_dim)
    all_keys = jnp.concatenate([live_keys, prev_keys, stretch_keys], axis=1)
    all_values = jnp.concatenate([live_values, prev_values, stretch_values], axis=1)
    query_rows = queries.reshape(kv_dev, q_per_kv * tok_dev, head_dim)
    step_rows = min(512, q_per_kv * tok_dev)
    columns = jnp.arange(span_cols + 2 * tok_dev, dtype=jnp.int32)

    def one_head(packed):
        q_head, k_head, v_head = packed
        q_steps = q_head.reshape(-1, step_rows, head_dim)
        starts = jnp.arange(q_steps.shape[0], dtype=jnp.int32) * step_rows

        def one_step(packed_block_step):
            q_block, first_row = packed_block_step
            position = (first_row + jnp.arange(step_rows, dtype=jnp.int32)) % tok_dev
            cache_part = columns[None, :] < span_cols
            earlier_part = (
                (columns[None, :] >= span_cols)
                & (columns[None, :] < span_cols + tok_dev)
                & (columns[None, :] - span_cols > position[:, None])
                & (ctx_index > 0)
            )
            own_part = (columns[None, :] >= span_cols + tok_dev) & (
                columns[None, :] - span_cols - tok_dev <= position[:, None]
            )
            return attend(q_block, k_head, v_head, cache_part | earlier_part | own_part)

        return lax.map(one_step, (q_steps, starts)).reshape(q_per_kv * tok_dev, head_dim)

    result = lax.map(one_head, (query_rows, all_keys, all_values))
    return result.reshape(kv_dev * q_per_kv, tok_dev, head_dim)


def solution(mesh):
    placed = (
        P(("head", "tp"), ("groups", "ctx"), None),
        P(("head", "tp"), ("groups", "ctx"), None),
        P(("head", "tp"), ("groups", "ctx"), None),
        P(("head", "tp"), ("groups", "ctx"), None),
        P(("head", "tp"), ("groups", "ctx"), None),
        P("groups", None, None),
        P("groups"),
    )
    return jax.shard_map(
        shards,
        mesh=mesh,
        in_specs=placed,
        out_specs=P(("head", "tp"), ("groups", "ctx"), None),
        check_vma=False,
    )
```

profile of v0, /device:TPU:0, one launch (start us, length us, event | category | flops | bytes accessed | tf_op | source)
XLA Modules:
  0.0 363.8 jit_solution(13856905821156815247)
XLA Ops:
  7.9 3.9 %gather_fusion.5 = bf16[32,256,128]{2,1,0:T(8,128)(2,1)} fusion(bf16[2,16,256,128]{3,2,1,0:T(8,128)(2,1)} %bitcast.67, s32[32]{0:T(128)S(1)} %reshape.259), kind=kCustom, calls=%fused_computation.5 | custom fusion | bytes 4194560 | tf_op jit(solution)/shard_map/vmap()/gather | solution.py:43
  11.9 3.2 broadcast_select_fusion
  16.7 6.4 %all-to-all-start = ((bf16[2,16,256,128]{3,2,0,1:T(8,128)(2,1)}), bf16[2,16,256,128]{3,2,0,1:T(8,128)(2,1)S(1)}, u32[]{:S(2)}, u32[]{:S(2)}) async-start(bf16[2,16,256,128]{3,2,0,1:T(8,128)(2,1)} %copy.18), calls=%async_computation | async-start | bytes 4194304 | tf_op jit(solution)/shard_map/all_to_all | solution.py:111
  23.1 3.1 copy.19
  26.2 45.1 %all-to-all-done = bf16[2,16,256,128]{3,2,0,1:T(8,128)(2,1)S(1)} async-done(((bf16[2,16,256,128]{3,2,0,1:T(8,128)(2,1)}), bf16[2,16,256,128]{3,2,0,1:T(8,128)(2,1)S(1)}, u32[]{:S(2)}, u32[]{:S(2)}) %all-to-all-start) | async-done | bytes 2097184 | tf_op jit(solution)/shard_map/all_to_all | solution.py:111
  71.3 4.5 %all-to-all-start.1 = ((bf16[2,16,256,128]{3,2,0,1:T(8,128)(2,1)}), bf16[2,16,256,128]{3,2,0,1:T(8,128)(2,1)}, u32[]{:S(2)}, u32[]{:S(2)}) async-start(bf16[2,16,256,128]{3,2,0,1:T(8,128)(2,1)} %copy.19), calls=%async_computation.1 | async-start | bytes 4194304 | tf_op jit(solution)/shard_map/all_to_all | solution.py:112
  80.5 43.2 %all-to-all-done.1 = bf16[2,16,256,128]{3,2,0,1:T(8,128)(2,1)} async-done(((bf16[2,16,256,128]{3,2,0,1:T(8,128)(2,1)}), bf16[2,16,256,128]{3,2,0,1:T(8,128)(2,1)}, u32[]{:S(2)}, u32[]{:S(2)}) %all-to-all-start.1) | async-done | bytes 2097184 | tf_op jit(solution)/shard_map/all_to_all | solution.py:112
  123.7 3.7 %gather_fusion.6 = bf16[32,256,128]{2,1,0:T(8,128)(2,1)} fusion(bf16[2,16,256,128]{3,2,0,1:T(8,128)(2,1)} %all-to-all-done.1, s32[32]{0:T(128)S(1)} %reshape.265), kind=kCustom, calls=%fused_computation.6 | custom fusion | bytes 4194560 | tf_op jit(solution)/shard_map/vmap()/gather | solution.py:43
  127.4 3.9 %collective-permute-start.3 = (bf16[2,256,128]{2,1,0:T(8,128)(2,1)S(1)}, bf16[2,256,128]{2,1,0:T(8,128)(2,1)S(1)}, u32[]{:S(2)}, u32[]{:S(2)}) collective-permute-start(bf16[2,256,128]{2,1,0:T(8,128)(2,1)S(1)} %copy-done.5), channel_id=1, source_target_pairs={{0,4},{4,8},{8,12},{1,5},{5,9},{9,13},{2,6},{6,10},{10,14},{3,7},{... | collective-permute-start | bytes 393224 | tf_op jit(solution)/shard_map/ppermute | solution.py:14
  131.4 2.6 collective-permute-start.1
  134.0 24.2 %collective-permute-done = bf16[2,16,256,128]{3,2,1,0:T(8,128)(2,1)} collective-permute-done((bf16[2,16,256,128]{3,2,1,0:T(8,128)(2,1)S(1)}, bf16[2,16,256,128]{3,2,1,0:T(8,128)(2,1)}, u32[]{:S(2)}, u32[]{:S(2)}) %collective-permute-start) | collective-permute-done | bytes 2097184 | tf_op jit(solution)/shard_map/ppermute | solution.py:28
  158.2 43.1 %collective-permute-done.2 = bf16[2,16,256,128]{3,2,1,0:T(8,128)(2,1)} collective-permute-done((bf16[2,16,256,128]{3,2,1,0:T(8,128)(2,1)}, bf16[2,16,256,128]{3,2,1,0:T(8,128)(2,1)}, u32[]{:S(2)}, u32[]{:S(2)}) %collective-permute-start.2) | collective-permute-done | bytes 2097184 | tf_op jit(solution)/shard_map/ppermute | solution.py:28
  201.3 3.1 broadcast_select_fusion.3
  204.9 10.0 %pad_maximum_fusion.1 = bf16[2,8704,128]{2,1,0:T(8,128)(2,1)} fusion(bf16[2,256,128]{2,1,0:T(8,128)(2,1)S(1)} %copy-done.5, bf16[2,256,128]{2,1,0:T(8,128)(2,1)S(1)} %collective-permute-done.3, bf16[2,8192,128]{2,1,0:T(8,128)(2,1)S(1)} %bitcast.56), kind=kLoop, calls=%fused_computation.36 | loop fusion | flops 13369344 | bytes 8912896 | tf_op jit(solution)/shard_map/concatenate | solution.py:130
  215.3 9.9 %pad_maximum_fusion = bf16[2,8704,128]{2,1,0:T(8,128)(2,1)} fusion(bf16[2,256,128]{2,1,0:T(8,128)(2,1)S(1)} %copy-done.6, bf16[2,256,128]{2,1,0:T(8,128)(2,1)S(1)} %collective-permute-done.1, bf16[2,8192,128]{2,1,0:T(8,128)(2,1)S(1)} %bitcast.57), kind=kLoop, calls=%fused_computation.35 | loop fusion | flops 13369344 | bytes 8912896 | tf_op jit(solution)/shard_map/concatenate | solution.py:129
  225.2 136.7 %while.49 = (s32[]{:T(128)}, bf16[2,1024,128]{2,1,0:T(8,128)(2,1)S(1)}, bf16[2,1024,128]{2,1,0:T(8,128)(2,1)S(1)}, bf16[2,8704,128]{2,1,0:T(8,128)(2,1)}, bf16[2...) while((s32[]{:T(128)}, ...), condition=%wide.region_10.11_spmd.clone.clone, body=%wide.region_5.10_spmd.clone.clone.sunk | while | flops 2344288768 | bytes 68473648 | solution.py:157
  225.2 3.9 %dynamic-slice_bitcast_fusion.3 = (bf16[8704,128]{1,0:T(8,128)(2,1)}, bf16[8704,128]{1,0:T(8,128)(2,1)}) fusion(bf16[2,8704,128]{2,1,0:T(8,128)(2,1)} %get-tuple-element.681, s32[]{:T(128)} %get-tuple-element.668, bf16[2,8704,128]{2,1,0:T(8,128)(2,1)} %get-tuple-element.680), kind=kLoop, calls=%fused_computation.30.clone.1 | loop fusion | bytes 8912900 | tf_op jit(solution)/shard_map/while/body/jit(dynamic_index_in_dim)/squeeze | solution.py:157
  229.2 64.4 %while.50 = (s32[]{:T(128)}, bf16[2,512,128]{2,1,0:T(8,128)(2,1)S(1)}, s32[8704]{0:T(1024)S(1)}, s32[2]{0:T(128)S(1)}, pred[]{:T(512)}, /*index=5*/bf16[2,512,12...) while((s32[]{:T(128)}, ...), condition=%wide.region_9.9_spmd.clone, body=%wide.region_6.8_spmd.clone.sunk | while | flops 2344288768 | bytes 58477172 | solution.py:155
  230.4 13.1 %fusion.43 = (f32[512]{0:T(512)S(1)}, f32[512,8704]{1,0:T(8,128)}) fusion(bf16[8704,128]{1,0:T(8,128)(2,1)} %get-tuple-element.656, bf16[2,512,128]{2,1,0:T(8,128)(2,1)S(1)} %get-tuple-element.655, s32[]{:T(128)} %get-tuple-element.641, s32[8704]{0:T(1024)S(1)} %get-tuple-element.625, pred[8704]{0:T(1024)(128)(4,1)S(1)} %get-tuple-element.626, ...), kind=kOutput, calls=%fused_computation.75.clone.1 | convolution fusion | flops 1185414656 | bytes 20290564 | tf_op jit(solution)/shard_map/while/body/eval_jaxpr/while/body/eval_jaxpr/rd,kd->rk/dot_general | solution.py:51
  243.5 8.5 %fusion.44 = f32[512]{0:T(512)S(1)} fusion(f32[512,8704]{1,0:T(8,128)} %get-tuple-element.630, f32[512]{0:T(512)S(1)} %get-tuple-element.631), kind=kLoop, calls=%fused_computation.10.clone.1 | loop fusion | flops 8912384 | bytes 17829888 | tf_op jit(solution)/shard_map/while/body/eval_jaxpr/while/body/eval_jaxpr/reduce_sum | solution.py:58
  252.1 9.3 %fusion.45 = bf16[2,512,128]{2,1,0:T(8,128)(2,1)S(1)} fusion(bf16[2,512,128]{2,1,0:T(8,128)(2,1)S(1)} %get-tuple-element.642, s32[]{:T(128)} %get-tuple-element.641, bf16[8704,128]{1,0:T(8,128)(2,1)} %get-tuple-element.657, f32[512,8704]{1,0:T(8,128)} %get-tuple-element.630, f32[512]{0:T(512)S(1)} %get-tuple-element.631, f32[512]{0:T(512)S(1)} %fusion.44), kind=kOutput, calls=%fused_computation.17.clone.1 | convolution fusion | flops 1149894656 | bytes 20189188 | tf_op jit(solution)/shard_map/while/body/eval_jaxpr/while/body/eval_jaxpr/rk,kd->rd/dot_general | solution.py:59
  262.6 13.1 %fusion.43 = (f32[512]{0:T(512)S(1)}, f32[512,8704]{1,0:T(8,128)}) fusion(bf16[8704,128]{1,0:T(8,128)(2,1)} %get-tuple-element.656, bf16[2,512,128]{2,1,0:T(8,128)(2,1)S(1)} %get-tuple-element.655, s32[]{:T(128)} %get-tuple-element.641, s32[8704]{0:T(1024)S(1)} %get-tuple-element.625, pred[8704]{0:T(1024)(128)(4,1)S(1)} %get-tuple-element.626, ...), kind=kOutput, calls=%fused_computation.75.clone.1 | convolution fusion | flops 1185414656 | bytes 20290564 | tf_op jit(solution)/shard_map/while/body/eval_jaxpr/while/body/eval_jaxpr/rd,kd->rk/dot_general | solution.py:51
  275.7 8.5 %fusion.44 = f32[512]{0:T(512)S(1)} fusion(f32[512,8704]{1,0:T(8,128)} %get-tuple-element.630, f32[512]{0:T(512)S(1)} %get-tuple-element.631), kind=kLoop, calls=%fused_computation.10.clone.1 | loop fusion | flops 8912384 | bytes 17829888 | tf_op jit(solution)/shard_map/while/body/eval_jaxpr/while/body/eval_jaxpr/reduce_sum | solution.py:58
  284.2 9.3 %fusion.45 = bf16[2,512,128]{2,1,0:T(8,128)(2,1)S(1)} fusion(bf16[2,512,128]{2,1,0:T(8,128)(2,1)S(1)} %get-tuple-element.642, s32[]{:T(128)} %get-tuple-element.641, bf16[8704,128]{1,0:T(8,128)(2,1)} %get-tuple-element.657, f32[512,8704]{1,0:T(8,128)} %get-tuple-element.630, f32[512]{0:T(512)S(1)} %get-tuple-element.631, f32[512]{0:T(512)S(1)} %fusion.44), kind=kOutput, calls=%fused_computation.17.clone.1 | convolution fusion | flops 1149894656 | bytes 20189188 | tf_op jit(solution)/shard_map/while/body/eval_jaxpr/while/body/eval_jaxpr/rk,kd->rd/dot_general | solution.py:59
  293.6 3.9 %dynamic-slice_bitcast_fusion.3 = (bf16[8704,128]{1,0:T(8,128)(2,1)}, bf16[8704,128]{1,0:T(8,128)(2,1)}) fusion(bf16[2,8704,128]{2,1,0:T(8,128)(2,1)} %get-tuple-element.681, s32[]{:T(128)} %get-tuple-element.668, bf16[2,8704,128]{2,1,0:T(8,128)(2,1)} %get-tuple-element.680), kind=kLoop, calls=%fused_computation.30.clone.1 | loop fusion | bytes 8912900 | tf_op jit(solution)/shard_map/while/body/jit(dynamic_index_in_dim)/squeeze | solution.py:157
  297.5 64.4 %while.50 = (s32[]{:T(128)}, bf16[2,512,128]{2,1,0:T(8,128)(2,1)S(1)}, s32[8704]{0:T(1024)S(1)}, s32[2]{0:T(128)S(1)}, pred[]{:T(512)}, /*index=5*/bf16[2,512,12...) while((s32[]{:T(128)}, ...), condition=%wide.region_9.9_spmd.clone, body=%wide.region_6.8_spmd.clone.sunk | while | flops 2344288768 | bytes 58477172 | solution.py:155
  298.8 13.1 %fusion.43 = (f32[512]{0:T(512)S(1)}, f32[512,8704]{1,0:T(8,128)}) fusion(bf16[8704,128]{1,0:T(8,128)(2,1)} %get-tuple-element.656, bf16[2,512,128]{2,1,0:T(8,128)(2,1)S(1)} %get-tuple-element.655, s32[]{:T(128)} %get-tuple-element.641, s32[8704]{0:T(1024)S(1)} %get-tuple-element.625, pred[8704]{0:T(1024)(128)(4,1)S(1)} %get-tuple-element.626, ...), kind=kOutput, calls=%fused_computation.75.clone.1 | convolution fusion | flops 1185414656 | bytes 20290564 | tf_op jit(solution)/shard_map/while/body/eval_jaxpr/while/body/eval_jaxpr/rd,kd->rk/dot_general | solution.py:51
  311.9 8.5 %fusion.44 = f32[512]{0:T(512)S(1)} fusion(f32[512,8704]{1,0:T(8,128)} %get-tuple-element.630, f32[512]{0:T(512)S(1)} %get-tuple-element.631), kind=kLoop, calls=%fused_computation.10.clone.1 | loop fusion | flops 8912384 | bytes 17829888 | tf_op jit(solution)/shard_map/while/body/eval_jaxpr/while/body/eval_jaxpr/reduce_sum | solution.py:58
  320.4 9.3 %fusion.45 = bf16[2,512,128]{2,1,0:T(8,128)(2,1)S(1)} fusion(bf16[2,512,128]{2,1,0:T(8,128)(2,1)S(1)} %get-tuple-element.642, s32[]{:T(128)} %get-tuple-element.641, bf16[8704,128]{1,0:T(8,128)(2,1)} %get-tuple-element.657, f32[512,8704]{1,0:T(8,128)} %get-tuple-element.630, f32[512]{0:T(512)S(1)} %get-tuple-element.631, f32[512]{0:T(512)S(1)} %fusion.44), kind=kOutput, calls=%fused_computation.17.clone.1 | convolution fusion | flops 1149894656 | bytes 20189188 | tf_op jit(solution)/shard_map/while/body/eval_jaxpr/while/body/eval_jaxpr/rk,kd->rd/dot_general | solution.py:59
  331.0 13.1 %fusion.43 = (f32[512]{0:T(512)S(1)}, f32[512,8704]{1,0:T(8,128)}) fusion(bf16[8704,128]{1,0:T(8,128)(2,1)} %get-tuple-element.656, bf16[2,512,128]{2,1,0:T(8,128)(2,1)S(1)} %get-tuple-element.655, s32[]{:T(128)} %get-tuple-element.641, s32[8704]{0:T(1024)S(1)} %get-tuple-element.625, pred[8704]{0:T(1024)(128)(4,1)S(1)} %get-tuple-element.626, ...), kind=kOutput, calls=%fused_computation.75.clone.1 | convolution fusion | flops 1185414656 | bytes 20290564 | tf_op jit(solution)/shard_map/while/body/eval_jaxpr/while/body/eval_jaxpr/rd,kd->rk/dot_general | solution.py:51
  344.1 8.5 %fusion.44 = f32[512]{0:T(512)S(1)} fusion(f32[512,8704]{1,0:T(8,128)} %get-tuple-element.630, f32[512]{0:T(512)S(1)} %get-tuple-element.631), kind=kLoop, calls=%fused_computation.10.clone.1 | loop fusion | flops 8912384 | bytes 17829888 | tf_op jit(solution)/shard_map/while/body/eval_jaxpr/while/body/eval_jaxpr/reduce_sum | solution.py:58
  352.6 9.3 %fusion.45 = bf16[2,512,128]{2,1,0:T(8,128)(2,1)S(1)} fusion(bf16[2,512,128]{2,1,0:T(8,128)(2,1)S(1)} %get-tuple-element.642, s32[]{:T(128)} %get-tuple-element.641, bf16[8704,128]{1,0:T(8,128)(2,1)} %get-tuple-element.657, f32[512,8704]{1,0:T(8,128)} %get-tuple-element.630, f32[512]{0:T(512)S(1)} %get-tuple-element.631, f32[512]{0:T(512)S(1)} %fusion.44), kind=kOutput, calls=%fused_computation.17.clone.1 | convolution fusion | flops 1149894656 | bytes 20189188 | tf_op jit(solution)/shard_map/while/body/eval_jaxpr/while/body/eval_jaxpr/rk,kd->rd/dot_general | solution.py:59
  (75 shorter events, 22.1 us)
Async XLA Ops:
  0.0 5.8 %copy-start = (bf16[2,4096,128]{2,1,0:T(8,128)(2,1)S(1)}, bf16[2,4096,128]{2,1,0:T(8,128)(2,1)}, u32[]{:S(2)}) copy-start(bf16[2,4096,128]{2,1,0:T(8,128)(2,1)} %param.19) | copy-start | bytes 6291460
  7.9 4.0 %copy-start.3 = (bf16[32,256,128]{2,1,0:T(8,128)(2,1)S(1)}, bf16[32,256,128]{2,1,0:T(8,128)(2,1)}, u32[]{:S(2)}) copy-start(bf16[32,256,128]{2,1,0:T(8,128)(2,1)} %gather_fusion.3) | copy-start | bytes 6291460
  16.7 54.6 %all-to-all-start = ((bf16[2,16,256,128]{3,2,0,1:T(8,128)(2,1)}), bf16[2,16,256,128]{3,2,0,1:T(8,128)(2,1)S(1)}, u32[]{:S(2)}, u32[]{:S(2)}) async-start(bf16[2,16,256,128]{3,2,0,1:T(8,128)(2,1)} %copy.18), calls=%async_computation | async-start | bytes 4194304 | tf_op jit(solution)/shard_map/all_to_all | solution.py:111
  71.3 4.5 %copy-start.2 = (bf16[2,16,256,128]{3,2,0,1:T(8,128)(2,1)}, bf16[2,16,256,128]{3,2,0,1:T(8,128)(2,1)S(1)}, u32[]{:S(2)}) copy-start(bf16[2,16,256,128]{3,2,0,1:T(8,128)(2,1)S(1)} %all-to-all-done) | copy-start | bytes 6291460
  71.3 52.4 %all-to-all-start.1 = ((bf16[2,16,256,128]{3,2,0,1:T(8,128)(2,1)}), bf16[2,16,256,128]{3,2,0,1:T(8,128)(2,1)}, u32[]{:S(2)}, u32[]{:S(2)}) async-start(bf16[2,16,256,128]{3,2,0,1:T(8,128)(2,1)} %copy.19), calls=%async_computation.1 | async-start | bytes 4194304 | tf_op jit(solution)/shard_map/all_to_all | solution.py:112
  75.9 51.5 %copy-start.5 = (bf16[2,256,128]{2,1,0:T(8,128)(2,1)S(1)}, bf16[2,256,128]{2,1,0:T(8,128)(2,1)}, u32[]{:S(2)}) copy-start(bf16[2,256,128]{2,1,0:T(8,128)(2,1)} %param.18) | copy-start | bytes 393220
  75.9 55.5 %copy-start.6 = (bf16[2,256,128]{2,1,0:T(8,128)(2,1)S(1)}, bf16[2,256,128]{2,1,0:T(8,128)(2,1)}, u32[]{:S(2)}) copy-start(bf16[2,256,128]{2,1,0:T(8,128)(2,1)} %param.17) | copy-start | bytes 393220
  78.5 79.7 %collective-permute-start = (bf16[2,16,256,128]{3,2,1,0:T(8,128)(2,1)S(1)}, bf16[2,16,256,128]{3,2,1,0:T(8,128)(2,1)}, u32[]{:S(2)}, u32[]{:S(2)}) collective-permute-start(bf16[2,16,256,128]{3,2,1,0:T(8,128)(2,1)S(1)} %bitcast.58), channel_id=1, source_target_pairs={{0,4},{4,0},{8,12},{12,8},{1,5},{5,1},{9,13},{13,9},{2,6},{6,2},{1... | collective-permute-start | bytes 6291464 | tf_op jit(solution)/shard_map/ppermute | solution.py:28
  127.4 73.9 %collective-permute-start.2 = (bf16[2,16,256,128]{3,2,1,0:T(8,128)(2,1)}, bf16[2,16,256,128]{3,2,1,0:T(8,128)(2,1)}, u32[]{:S(2)}, u32[]{:S(2)}) collective-permute-start(bf16[2,16,256,128]{3,2,1,0:T(8,128)(2,1)} %bitcast.60), channel_id=1, source_target_pairs={{0,4},{4,0},{8,12},{12,8},{1,5},{5,1},{9,13},{13,9},{2,6},{6,2},{1... | collective-permute-start | bytes 6291464 | tf_op jit(solution)/shard_map/ppermute | solution.py:28
  127.4 77.5 %collective-permute-start.3 = (bf16[2,256,128]{2,1,0:T(8,128)(2,1)S(1)}, bf16[2,256,128]{2,1,0:T(8,128)(2,1)S(1)}, u32[]{:S(2)}, u32[]{:S(2)}) collective-permute-start(bf16[2,256,128]{2,1,0:T(8,128)(2,1)S(1)} %copy-done.5), channel_id=1, source_target_pairs={{0,4},{4,8},{8,12},{1,5},{5,9},{9,13},{2,6},{6,10},{10,14},{3,7},{... | collective-permute-start | bytes 393224 | tf_op jit(solution)/shard_map/ppermute | solution.py:14
  131.4 83.9 %collective-permute-start.1 = (bf16[2,256,128]{2,1,0:T(8,128)(2,1)S(1)}, bf16[2,256,128]{2,1,0:T(8,128)(2,1)S(1)}, u32[]{:S(2)}, u32[]{:S(2)}) collective-permute-start(bf16[2,256,128]{2,1,0:T(8,128)(2,1)S(1)} %copy-done.6), channel_id=1, source_target_pairs={{0,4},{4,8},{8,12},{1,5},{5,9},{9,13},{2,6},{6,10},{10,14},{3,7},{... | collective-permute-start | bytes 393224 | tf_op jit(solution)/shard_map/ppermute | solution.py:14
  215.3 9.9 %copy-start.4 = (bf16[8,256,128]{2,1,0:T(8,128)(2,1)S(1)}, bf16[8,256,128]{2,1,0:T(8,128)(2,1)}, u32[]{:S(2)}) copy-start(bf16[8,256,128]{2,1,0:T(8,128)(2,1)} %param.16) | copy-start | bytes 1572868
  362.0 0.8 copy-start.7
  362.0 1.8 copy-start.1
where the time goes:
time: 365 us; the launch traced here: 364 us
  waiting for transfers between devices  156 us (43%)
  matrix products  89.4 us (24%)
  other arithmetic  67.8 us (19%)
  local copies, waits for them, and re-layouts  31.2 us (9%)
  starting transfers between devices  19.4 us (5%)
    ppermute x2, waiting for transfers between devices, partner(): return lax.ppermute(value, axis, pairs)  67.3 us
    dot_general x4, matrix products, attend(): jnp.einsum('rd,kd->rk', query_rows, all_keys, preferred_element_type=jnp....  52.3 us
    all_to_all x1, waiting for transfers between devices, shards(): lax.all_to_all(sent_keys, 'ctx', split_axis=1, concat_axis=1, tiled=True)  45.1 us
    all_to_all x1, waiting for transfers between devices, shards(): lax.all_to_all(sent_values, 'ctx', split_axis=1, concat_axis=1, tiled=True)  43.2 us
    dot_general x4, matrix products, attend(): jnp.einsum('rk,kd->rd', weights.astype(jnp.bfloat16), all_values, preferr...  37.1 us
    reduce_sum x4, other arithmetic, attend(): weight_sum = jnp.sum(weights, axis=-1, keepdims=True)  34.2 us
    gather x6, local copies, waits for them, and re-layouts, pick_rows(): return source[indices]  12.5 us
    concatenate x1, other arithmetic, shards(): jnp.concatenate([live_values, prev_values, stretch_values], axis=1)  9.97 us
  transfers between devices with their start and end apart: 6, of which 4 were waited for; matrix products, arithmetic and copies ran while one was open for 6% of the time, Pallas kernels for 0%

commit v1 on v0

--- a/solution.py
+++ b/solution.py
@@ -6,6 +6,20 @@
 
 BLOCK = 512
 TOPK = 16
+
+
+def play_scenes(unit, ndim_at, local):
+    value_now = unit.shape
+    y_new = unit.reshape(
+        *value_now[:ndim_at], local, value_now[ndim_at] // local, *value_now[ndim_at + 1 :]
+    )
+    return jnp.moveaxis(y_new, ndim_at, 0)
+
+
+def ratios_form(own_rows, along_dim):
+    u1 = list(own_rows.shape[1:])
+    u1[along_dim] *= own_rows.shape[0]
+    return jnp.moveaxis(own_rows, 0, along_dim).reshape(u1)
 
 
 def shifted(value, axis, by):
@@ -107,9 +121,22 @@
     sent_values = jnp.where(
         usable[:, :, None, None], take_blocks(value_halves, half_index), 0
     ).astype(jnp.bfloat16)
+
+    def list_joints(target, chip_axis, incoming_x, block_here):
+        u_next, earlier = (lax.psum(1, chip_axis), lax.axis_index(chip_axis))
+        after = play_scenes(incoming_x, block_here, u_next)
+        lanes = [after[earlier]]
+        i0 = 1
+        while i0 < u_next:
+            wide_out = after[earlier ^ i0]
+            lanes.append(lax.ppermute(wide_out, chip_axis, [(b, b ^ i0) for b in range(u_next)]))
+            i0 += 1
+        after = jnp.stack(lanes)[earlier ^ jnp.arange(u_next)]
+        return ratios_form(after, target)
+
     got_keys, got_values = (
         lax.all_to_all(sent_keys, "ctx", split_axis=1, concat_axis=1, tiled=True),
-        lax.all_to_all(sent_values, "ctx", split_axis=1, concat_axis=1, tiled=True),
+        list_joints(1, "ctx", sent_values, 1),
     )
     mine_keys = take_blocks(got_keys, my_slot)
     mine_values = take_blocks(got_values, my_slot)

time: 365 us -> 375 us (1.027)
  starting transfers between devices: 19.4 us -> 27.6 us
    ppermute x0 -> x3, waiting for transfers between devices: none -> 75.3 us  [list_joints(): lax.ppermute(wide_out, chip_axis, [(b, b ^ i0) for b in range(u_next)])]
    all_to_all x1, waiting for transfers between devices: 45.1 us -> 0.01 us  [shards(): lax.all_to_all(sent_keys, 'ctx', split_axis=1, concat_axis=1, tiled=True)]
    all_to_all x1 -> x0, waiting for transfers between devices: 43.2 us -> none  [shards(): lax.all_to_all(sent_values, 'ctx', split_axis=1, concat_axis=1, tiled=True)]
    ppermute x2, waiting for transfers between devices: 67.3 us -> 80.7 us  [partner(): return lax.ppermute(value, axis, pairs)]
    ppermute x2, starting transfers between devices: 2.02 us -> 10.2 us  [partner(): return lax.ppermute(value, axis, pairs)]
    ppermute x0 -> x3, starting transfers between devices: none -> 4.53 us  [list_joints(): lax.ppermute(wide_out, chip_axis, [(b, b ^ i0) for b in range(u_next)])]
    all_to_all x1 -> x0, starting transfers between devices: 4.47 us -> none  [shards(): lax.all_to_all(sent_values, 'ctx', split_axis=1, concat_axis=1, tiled=True)]
  transfers between devices with their start and end apart: 6 -> 8, of which waited for: 4 -> 4; matrix products, arithmetic and copies ran while one was open for 6% -> 8% of each run, Pallas kernels for 0% -> 0%
where the time goes in v1:
time: 375 us
  waiting for transfers between devices  156 us (42%)
  matrix products  89.4 us (24%)
  other arithmetic  68.1 us (18%)
  local copies, waits for them, and re-layouts  32.9 us (9%)
  starting transfers between devices  27.6 us (7%)
    ppermute x2, waiting for transfers between devices, partner(): return lax.ppermute(value, axis, pairs)  80.7 us
    ppermute x3, waiting for transfers between devices, list_joints(): lax.ppermute(wide_out, chip_axis, [(b, b ^ i0) for b in range(u_next)])  75.3 us
    dot_general x4, matrix products, attend(): jnp.einsum('rd,kd->rk', query_rows, all_keys, preferred_element_type=jnp....  52.3 us
    dot_general x4, matrix products, attend(): jnp.einsum('rk,kd->rd', weights.astype(jnp.bfloat16), all_values, preferr...  37.1 us
    reduce_sum x4, other arithmetic, attend(): weight_sum = jnp.sum(weights, axis=-1, keepdims=True)  34.2 us
    gather x6, local copies, waits for them, and re-layouts, pick_rows(): return source[indices]  11.1 us
    ppermute x2, starting transfers between devices, partner(): return lax.ppermute(value, axis, pairs)  10.2 us
    concatenate x1, other arithmetic, shards(): jnp.concatenate([live_values, prev_values, stretch_values], axis=1)  9.97 us
  transfers between devices with their start and end apart: 8, of which 4 were waited for; matrix products, arithmetic and copies ran while one was open for 8% of the time, Pallas kernels for 0%

profile of v1, /device:TPU:0, one launch (start us, length us, event | category | flops | bytes accessed | tf_op | source)
XLA Modules:
  0.0 374.5 jit_solution(12109127555479118434)
XLA Ops:
  11.4 6.4 %all-to-all-start = ((bf16[2,16,256,128]{3,2,0,1:T(8,128)(2,1)}), bf16[2,16,256,128]{3,2,0,1:T(8,128)(2,1)}, u32[]{:S(2)}, u32[]{:S(2)}) async-start(bf16[2,16,256,128]{3,2,0,1:T(8,128)(2,1)} %copy.22), calls=%async_computation | async-start | bytes 4194304 | tf_op jit(solution)/shard_map/all_to_all | solution.py:138
  17.8 2.5 gather_fusion.6
  25.4 38.7 %collective-permute-done.2 = bf16[2,4,256,128]{3,2,1,0:T(8,128)(2,1)S(1)} collective-permute-done((bf16[2,4,256,128]{3,2,1,0:T(8,128)(2,1)S(1)}, bf16[2,4,256,128]{3,2,1,0:T(8,128)(2,1)S(1)}, u32[]{:S(2)}, u32[]{:S(2)}) %collective-permute-start.2) | collective-permute-done | bytes 524320 | tf_op jit(solution)/shard_map/ppermute | solution.py:132
  64.0 36.6 %collective-permute-done.3 = bf16[2,4,256,128]{3,2,1,0:T(8,128)(2,1)S(1)} collective-permute-done((bf16[2,4,256,128]{3,2,1,0:T(8,128)(2,1)S(1)}, bf16[2,4,256,128]{3,2,1,0:T(8,128)(2,1)S(1)}, u32[]{:S(2)}, u32[]{:S(2)}) %collective-permute-start.3) | collective-permute-done | bytes 524320 | tf_op jit(solution)/shard_map/ppermute | solution.py:132
  105.0 3.2 copy.24
  108.2 2.5 gather_fusion.7
  110.8 10.2 %collective-permute-start.5 = (bf16[2,16,256,128]{3,2,1,0:T(8,128)(2,1)S(1)}, bf16[2,16,256,128]{3,2,1,0:T(8,128)(2,1)}, u32[]{:S(2)}, u32[]{:S(2)}) collective-permute-start(bf16[2,16,256,128]{3,2,1,0:T(8,128)(2,1)S(1)} %bitcast.77), channel_id=1, source_target_pairs={{0,4},{4,0},{8,12},{12,8},{1,5},{5,1},{9,13},{13,9},{2,6},{6,2},{1... | collective-permute-start | bytes 6291464 | tf_op jit(solution)/shard_map/ppermute | solution.py:42
  121.0 3.7 gather_fusion.5
  124.7 3.9 %collective-permute-start.6 = (bf16[2,256,128]{2,1,0:T(8,128)(2,1)S(1)}, bf16[2,256,128]{2,1,0:T(8,128)(2,1)S(1)}, u32[]{:S(2)}, u32[]{:S(2)}) collective-permute-start(bf16[2,256,128]{2,1,0:T(8,128)(2,1)S(1)} %copy-done.4), channel_id=1, source_target_pairs={{0,4},{4,8},{8,12},{1,5},{5,9},{9,13},{2,6},{6,10},{10,14},{3,7},{... | collective-permute-start | bytes 393224 | tf_op jit(solution)/shard_map/ppermute | solution.py:28
  128.6 2.7 collective-permute-start.1
  131.3 36.2 %collective-permute-done.5 = bf16[2,16,256,128]{3,2,1,0:T(8,128)(2,1)} collective-permute-done((bf16[2,16,256,128]{3,2,1,0:T(8,128)(2,1)S(1)}, bf16[2,16,256,128]{3,2,1,0:T(8,128)(2,1)}, u32[]{:S(2)}, u32[]{:S(2)}) %collective-permute-start.5) | collective-permute-done | bytes 2097184 | tf_op jit(solution)/shard_map/ppermute | solution.py:42
  167.6 44.5 %collective-permute-done = bf16[2,16,256,128]{3,2,1,0:T(8,128)(2,1)} collective-permute-done((bf16[2,16,256,128]{3,2,1,0:T(8,128)(2,1)}, bf16[2,16,256,128]{3,2,1,0:T(8,128)(2,1)}, u32[]{:S(2)}, u32[]{:S(2)}) %collective-permute-start) | collective-permute-done | bytes 2097184 | tf_op jit(solution)/shard_map/ppermute | solution.py:42
  212.0 3.1 broadcast_select_fusion.3
  215.6 10.0 %pad_maximum_fusion.1 = bf16[2,8704,128]{2,1,0:T(8,128)(2,1)} fusion(bf16[2,256,128]{2,1,0:T(8,128)(2,1)S(1)} %copy-done.4, bf16[2,256,128]{2,1,0:T(8,128)(2,1)S(1)} %collective-permute-done.6, bf16[2,8192,128]{2,1,0:T(8,128)(2,1)S(1)} %bitcast.75), kind=kLoop, calls=%fused_computation.37 | loop fusion | flops 13369344 | bytes 8912896 | tf_op jit(solution)/shard_map/concatenate | solution.py:157
  226.1 9.9 %pad_maximum_fusion = bf16[2,8704,128]{2,1,0:T(8,128)(2,1)} fusion(bf16[2,256,128]{2,1,0:T(8,128)(2,1)S(1)} %copy-done.5, bf16[2,256,128]{2,1,0:T(8,128)(2,1)S(1)} %collective-permute-done.1, bf16[2,8192,128]{2,1,0:T(8,128)(2,1)S(1)} %bitcast.76), kind=kLoop, calls=%fused_computation.36 | loop fusion | flops 13369344 | bytes 8912896 | tf_op jit(solution)/shard_map/concatenate | solution.py:156
  236.0 136.7 %while.49 = (s32[]{:T(128)}, bf16[2,1024,128]{2,1,0:T(8,128)(2,1)S(1)}, bf16[2,1024,128]{2,1,0:T(8,128)(2,1)S(1)}, bf16[2,8704,128]{2,1,0:T(8,128)(2,1)}, bf16[2...) while((s32[]{:T(128)}, ...), condition=%wide.region_10.11_spmd.clone.clone, body=%wide.region_5.10_spmd.clone.clone.sunk | while | flops 2344288768 | bytes 68473648 | solution.py:184
  236.0 3.9 %dynamic-slice_bitcast_fusion.7 = (bf16[8704,128]{1,0:T(8,128)(2,1)}, bf16[8704,128]{1,0:T(8,128)(2,1)}) fusion(bf16[2,8704,128]{2,1,0:T(8,128)(2,1)} %get-tuple-element.683, s32[]{:T(128)} %get-tuple-element.670, bf16[2,8704,128]{2,1,0:T(8,128)(2,1)} %get-tuple-element.682), kind=kLoop, calls=%fused_computation.31.clone.1 | loop fusion | bytes 8912900 | tf_op jit(solution)/shard_map/while/body/jit(dynamic_index_in_dim)/squeeze | solution.py:184
  239.9 64.4 %while.50 = (s32[]{:T(128)}, bf16[2,512,128]{2,1,0:T(8,128)(2,1)S(1)}, s32[8704]{0:T(1024)S(1)}, s32[2]{0:T(128)S(1)}, pred[]{:T(512)}, /*index=5*/bf16[2,512,12...) while((s32[]{:T(128)}, ...), condition=%wide.region_9.9_spmd.clone, body=%wide.region_6.8_spmd.clone.sunk | while | flops 2344288768 | bytes 58477172 | solution.py:182
  241.2 13.1 %fusion.44 = (f32[512]{0:T(512)S(1)}, f32[512,8704]{1,0:T(8,128)}) fusion(bf16[8704,128]{1,0:T(8,128)(2,1)} %get-tuple-element.658, bf16[2,512,128]{2,1,0:T(8,128)(2,1)S(1)} %get-tuple-element.657, s32[]{:T(128)} %get-tuple-element.643, s32[8704]{0:T(1024)S(1)} %get-tuple-element.627, pred[8704]{0:T(1024)(128)(4,1)S(1)} %get-tuple-element.628, ...), kind=kOutput, calls=%fused_computation.87.clone.1 | convolution fusion | flops 1185414656 | bytes 20290564 | tf_op jit(solution)/shard_map/while/body/eval_jaxpr/while/body/eval_jaxpr/rd,kd->rk/dot_general | solution.py:65
  254.3 8.5 %fusion.45 = f32[512]{0:T(512)S(1)} fusion(f32[512,8704]{1,0:T(8,128)} %get-tuple-element.632, f32[512]{0:T(512)S(1)} %get-tuple-element.633), kind=kLoop, calls=%fused_computation.11.clone.1 | loop fusion | flops 8912384 | bytes 17829888 | tf_op jit(solution)/shard_map/while/body/eval_jaxpr/while/body/eval_jaxpr/reduce_sum | solution.py:72
  262.8 9.3 %fusion.46 = bf16[2,512,128]{2,1,0:T(8,128)(2,1)S(1)} fusion(bf16[2,512,128]{2,1,0:T(8,128)(2,1)S(1)} %get-tuple-element.644, s32[]{:T(128)} %get-tuple-element.643, bf16[8704,128]{1,0:T(8,128)(2,1)} %get-tuple-element.659, f32[512,8704]{1,0:T(8,128)} %get-tuple-element.632, f32[512]{0:T(512)S(1)} %get-tuple-element.633, f32[512]{0:T(512)S(1)} %fusion.45), kind=kOutput, calls=%fused_computation.18.clone.1 | convolution fusion | flops 1149894656 | bytes 20189188 | tf_op jit(solution)/shard_map/while/body/eval_jaxpr/while/body/eval_jaxpr/rk,kd->rd/dot_general | solution.py:73
  273.4 13.1 %fusion.44 = (f32[512]{0:T(512)S(1)}, f32[512,8704]{1,0:T(8,128)}) fusion(bf16[8704,128]{1,0:T(8,128)(2,1)} %get-tuple-element.658, bf16[2,512,128]{2,1,0:T(8,128)(2,1)S(1)} %get-tuple-element.657, s32[]{:T(128)} %get-tuple-element.643, s32[8704]{0:T(1024)S(1)} %get-tuple-element.627, pred[8704]{0:T(1024)(128)(4,1)S(1)} %get-tuple-element.628, ...), kind=kOutput, calls=%fused_computation.87.clone.1 | convolution fusion | flops 1185414656 | bytes 20290564 | tf_op jit(solution)/shard_map/while/body/eval_jaxpr/while/body/eval_jaxpr/rd,kd->rk/dot_general | solution.py:65
  286.5 8.5 %fusion.45 = f32[512]{0:T(512)S(1)} fusion(f32[512,8704]{1,0:T(8,128)} %get-tuple-element.632, f32[512]{0:T(512)S(1)} %get-tuple-element.633), kind=kLoop, calls=%fused_computation.11.clone.1 | loop fusion | flops 8912384 | bytes 17829888 | tf_op jit(solution)/shard_map/while/body/eval_jaxpr/while/body/eval_jaxpr/reduce_sum | solution.py:72
  295.0 9.3 %fusion.46 = bf16[2,512,128]{2,1,0:T(8,128)(2,1)S(1)} fusion(bf16[2,512,128]{2,1,0:T(8,128)(2,1)S(1)} %get-tuple-element.644, s32[]{:T(128)} %get-tuple-element.643, bf16[8704,128]{1,0:T(8,128)(2,1)} %get-tuple-element.659, f32[512,8704]{1,0:T(8,128)} %get-tuple-element.632, f32[512]{0:T(512)S(1)} %get-tuple-element.633, f32[512]{0:T(512)S(1)} %fusion.45), kind=kOutput, calls=%fused_computation.18.clone.1 | convolution fusion | flops 1149894656 | bytes 20189188 | tf_op jit(solution)/shard_map/while/body/eval_jaxpr/while/body/eval_jaxpr/rk,kd->rd/dot_general | solution.py:73
  304.4 3.9 %dynamic-slice_bitcast_fusion.7 = (bf16[8704,128]{1,0:T(8,128)(2,1)}, bf16[8704,128]{1,0:T(8,128)(2,1)}) fusion(bf16[2,8704,128]{2,1,0:T(8,128)(2,1)} %get-tuple-element.683, s32[]{:T(128)} %get-tuple-element.670, bf16[2,8704,128]{2,1,0:T(8,128)(2,1)} %get-tuple-element.682), kind=kLoop, calls=%fused_computation.31.clone.1 | loop fusion | bytes 8912900 | tf_op jit(solution)/shard_map/while/body/jit(dynamic_index_in_dim)/squeeze | solution.py:184
  308.3 64.4 %while.50 = (s32[]{:T(128)}, bf16[2,512,128]{2,1,0:T(8,128)(2,1)S(1)}, s32[8704]{0:T(1024)S(1)}, s32[2]{0:T(128)S(1)}, pred[]{:T(512)}, /*index=5*/bf16[2,512,12...) while((s32[]{:T(128)}, ...), condition=%wide.region_9.9_spmd.clone, body=%wide.region_6.8_spmd.clone.sunk | while | flops 2344288768 | bytes 58477172 | solution.py:182
  309.6 13.1 %fusion.44 = (f32[512]{0:T(512)S(1)}, f32[512,8704]{1,0:T(8,128)}) fusion(bf16[8704,128]{1,0:T(8,128)(2,1)} %get-tuple-element.658, bf16[2,512,128]{2,1,0:T(8,128)(2,1)S(1)} %get-tuple-element.657, s32[]{:T(128)} %get-tuple-element.643, s32[8704]{0:T(1024)S(1)} %get-tuple-element.627, pred[8704]{0:T(1024)(128)(4,1)S(1)} %get-tuple-element.628, ...), kind=kOutput, calls=%fused_computation.87.clone.1 | convolution fusion | flops 1185414656 | bytes 20290564 | tf_op jit(solution)/shard_map/while/body/eval_jaxpr/while/body/eval_jaxpr/rd,kd->rk/dot_general | solution.py:65
  322.7 8.5 %fusion.45 = f32[512]{0:T(512)S(1)} fusion(f32[512,8704]{1,0:T(8,128)} %get-tuple-element.632, f32[512]{0:T(512)S(1)} %get-tuple-element.633), kind=kLoop, calls=%fused_computation.11.clone.1 | loop fusion | flops 8912384 | bytes 17829888 | tf_op jit(solution)/shard_map/while/body/eval_jaxpr/while/body/eval_jaxpr/reduce_sum | solution.py:72
  331.2 9.3 %fusion.46 = bf16[2,512,128]{2,1,0:T(8,128)(2,1)S(1)} fusion(bf16[2,512,128]{2,1,0:T(8,128)(2,1)S(1)} %get-tuple-element.644, s32[]{:T(128)} %get-tuple-element.643, bf16[8704,128]{1,0:T(8,128)(2,1)} %get-tuple-element.659, f32[512,8704]{1,0:T(8,128)} %get-tuple-element.632, f32[512]{0:T(512)S(1)} %get-tuple-element.633, f32[512]{0:T(512)S(1)} %fusion.45), kind=kOutput, calls=%fused_computation.18.clone.1 | convolution fusion | flops 1149894656 | bytes 20189188 | tf_op jit(solution)/shard_map/while/body/eval_jaxpr/while/body/eval_jaxpr/rk,kd->rd/dot_general | solution.py:73
  341.8 13.1 %fusion.44 = (f32[512]{0:T(512)S(1)}, f32[512,8704]{1,0:T(8,128)}) fusion(bf16[8704,128]{1,0:T(8,128)(2,1)} %get-tuple-element.658, bf16[2,512,128]{2,1,0:T(8,128)(2,1)S(1)} %get-tuple-element.657, s32[]{:T(128)} %get-tuple-element.643, s32[8704]{0:T(1024)S(1)} %get-tuple-element.627, pred[8704]{0:T(1024)(128)(4,1)S(1)} %get-tuple-element.628, ...), kind=kOutput, calls=%fused_computation.87.clone.1 | convolution fusion | flops 1185414656 | bytes 20290564 | tf_op jit(solution)/shard_map/while/body/eval_jaxpr/while/body/eval_jaxpr/rd,kd->rk/dot_general | solution.py:65
  354.8 8.5 %fusion.45 = f32[512]{0:T(512)S(1)} fusion(f32[512,8704]{1,0:T(8,128)} %get-tuple-element.632, f32[512]{0:T(512)S(1)} %get-tuple-element.633), kind=kLoop, calls=%fused_computation.11.clone.1 | loop fusion | flops 8912384 | bytes 17829888 | tf_op jit(solution)/shard_map/while/body/eval_jaxpr/while/body/eval_jaxpr/reduce_sum | solution.py:72
  363.4 9.3 %fusion.46 = bf16[2,512,128]{2,1,0:T(8,128)(2,1)S(1)} fusion(bf16[2,512,128]{2,1,0:T(8,128)(2,1)S(1)} %get-tuple-element.644, s32[]{:T(128)} %get-tuple-element.643, bf16[8704,128]{1,0:T(8,128)(2,1)} %get-tuple-element.659, f32[512,8704]{1,0:T(8,128)} %get-tuple-element.632, f32[512]{0:T(512)S(1)} %get-tuple-element.633, f32[512]{0:T(512)S(1)} %fusion.45), kind=kOutput, calls=%fused_computation.18.clone.1 | convolution fusion | flops 1149894656 | bytes 20189188 | tf_op jit(solution)/shard_map/while/body/eval_jaxpr/while/body/eval_jaxpr/rk,kd->rd/dot_general | solution.py:73
  (83 shorter events, 28.7 us)
Async XLA Ops:
  0.0 5.9 %copy-start = (bf16[2,4096,128]{2,1,0:T(8,128)(2,1)S(1)}, bf16[2,4096,128]{2,1,0:T(8,128)(2,1)}, u32[]{:S(2)}) copy-start(bf16[2,4096,128]{2,1,0:T(8,128)(2,1)} %param.19) | copy-start | bytes 6291460
  11.4 109.6 %all-to-all-start = ((bf16[2,16,256,128]{3,2,0,1:T(8,128)(2,1)}), bf16[2,16,256,128]{3,2,0,1:T(8,128)(2,1)}, u32[]{:S(2)}, u32[]{:S(2)}) async-start(bf16[2,16,256,128]{3,2,0,1:T(8,128)(2,1)} %copy.22), calls=%async_computation | async-start | bytes 4194304 | tf_op jit(solution)/shard_map/all_to_all | solution.py:138
  20.7 43.3 %collective-permute-start.2 = (bf16[2,4,256,128]{3,2,1,0:T(8,128)(2,1)S(1)}, bf16[2,4,256,128]{3,2,1,0:T(8,128)(2,1)S(1)}, u32[]{:S(2)}, u32[]{:S(2)}) collective-permute-start(bf16[2,4,256,128]{3,2,1,0:T(8,128)(2,1)S(1)} %get-tuple-element.506), channel_id=1, source_target_pairs={{0,4},{4,0},{8,12},{12,8},{1,5},{5,1},{9,13},{13,9},{2,6},{6,2},{1... | collective-permute-start | bytes 1572872 | tf_op jit(solution)/shard_map/ppermute | solution.py:132
  22.8 77.8 %collective-permute-start.3 = (bf16[2,4,256,128]{3,2,1,0:T(8,128)(2,1)S(1)}, bf16[2,4,256,128]{3,2,1,0:T(8,128)(2,1)S(1)}, u32[]{:S(2)}, u32[]{:S(2)}) collective-permute-start(bf16[2,4,256,128]{3,2,1,0:T(8,128)(2,1)S(1)} %get-tuple-element.505), channel_id=1, source_target_pairs={{0,8},{4,12},{8,0},{12,4},{1,9},{5,13},{9,1},{13,5},{2,10},{6,14},... | collective-permute-start | bytes 1572872 | tf_op jit(solution)/shard_map/ppermute | solution.py:132
  25.2 75.5 %collective-permute-start.4 = (bf16[2,4,256,128]{3,2,1,0:T(8,128)(2,1)S(1)}, bf16[2,4,256,128]{3,2,1,0:T(8,128)(2,1)}, u32[]{:S(2)}, u32[]{:S(2)}) collective-permute-start(bf16[2,4,256,128]{3,2,1,0:T(8,128)(2,1)S(1)} %get-tuple-element.504), channel_id=1, source_target_pairs={{0,12},{4,8},{8,4},{12,0},{1,13},{5,9},{9,5},{13,1},{2,14},{6,10},... | collective-permute-start | bytes 1572872 | tf_op jit(solution)/shard_map/ppermute | solution.py:132
  100.7 0.8 copy-start.3
  110.8 14.0 %copy-start.4 = (bf16[2,256,128]{2,1,0:T(8,128)(2,1)S(1)}, bf16[2,256,128]{2,1,0:T(8,128)(2,1)}, u32[]{:S(2)}) copy-start(bf16[2,256,128]{2,1,0:T(8,128)(2,1)} %param.18) | copy-start | bytes 393220
  110.8 17.9 %copy-start.5 = (bf16[2,256,128]{2,1,0:T(8,128)(2,1)S(1)}, bf16[2,256,128]{2,1,0:T(8,128)(2,1)}, u32[]{:S(2)}) copy-start(bf16[2,256,128]{2,1,0:T(8,128)(2,1)} %param.17) | copy-start | bytes 393220
  110.8 56.8 %collective-permute-start.5 = (bf16[2,16,256,128]{3,2,1,0:T(8,128)(2,1)S(1)}, bf16[2,16,256,128]{3,2,1,0:T(8,128)(2,1)}, u32[]{:S(2)}, u32[]{:S(2)}) collective-permute-start(bf16[2,16,256,128]{3,2,1,0:T(8,128)(2,1)S(1)} %bitcast.77), channel_id=1, source_target_pairs={{0,4},{4,0},{8,12},{12,8},{1,5},{5,1},{9,13},{13,9},{2,6},{6,2},{1... | collective-permute-start | bytes 6291464 | tf_op jit(solution)/shard_map/ppermute | solution.py:42
  124.7 87.3 %collective-permute-start = (bf16[2,16,256,128]{3,2,1,0:T(8,128)(2,1)}, bf16[2,16,256,128]{3,2,1,0:T(8,128)(2,1)}, u32[]{:S(2)}, u32[]{:S(2)}) collective-permute-start(bf16[2,16,256,128]{3,2,1,0:T(8,128)(2,1)} %bitcast.79), channel_id=1, source_target_pairs={{0,4},{4,0},{8,12},{12,8},{1,5},{5,1},{9,13},{13,9},{2,6},{6,2},{1... | collective-permute-start | bytes 6291464 | tf_op jit(solution)/shard_map/ppermute | solution.py:42
  124.7 90.9 %collective-permute-start.6 = (bf16[2,256,128]{2,1,0:T(8,128)(2,1)S(1)}, bf16[2,256,128]{2,1,0:T(8,128)(2,1)S(1)}, u32[]{:S(2)}, u32[]{:S(2)}) collective-permute-start(bf16[2,256,128]{2,1,0:T(8,128)(2,1)S(1)} %copy-done.4), channel_id=1, source_target_pairs={{0,4},{4,8},{8,12},{1,5},{5,9},{9,13},{2,6},{6,10},{10,14},{3,7},{... | collective-permute-start | bytes 393224 | tf_op jit(solution)/shard_map/ppermute | solution.py:28
  128.6 97.4 %collective-permute-start.1 = (bf16[2,256,128]{2,1,0:T(8,128)(2,1)S(1)}, bf16[2,256,128]{2,1,0:T(8,128)(2,1)S(1)}, u32[]{:S(2)}, u32[]{:S(2)}) collective-permute-start(bf16[2,256,128]{2,1,0:T(8,128)(2,1)S(1)} %copy-done.5), channel_id=1, source_target_pairs={{0,4},{4,8},{8,12},{1,5},{5,9},{9,13},{2,6},{6,10},{10,14},{3,7},{... | collective-permute-start | bytes 393224 | tf_op jit(solution)/shard_map/ppermute | solution.py:28
  226.1 9.9 %copy-start.2 = (bf16[8,256,128]{2,1,0:T(8,128)(2,1)S(1)}, bf16[8,256,128]{2,1,0:T(8,128)(2,1)}, u32[]{:S(2)}) copy-start(bf16[8,256,128]{2,1,0:T(8,128)(2,1)} %param.16) | copy-start | bytes 1572868
  372.7 0.8 copy-start.6
  372.7 1.8 copy-start.1
